TPU v7x, 256 devices: a whole 4x4x8 slice. The times are simulated.
256 devices in a mesh: section: 4 (over x), tp: 16 (over y, z_hi, core), dp: 4 (over z_lo).
Axes of the slice: x: 4, y: 4, z: 8 (z_hi: 2, z_lo: 4; z = z_hi * 4 + z_lo), core: 2. Of those that a mesh axis runs over, the one named last changes fastest.
Arguments:
- responses: bfloat16 [2048, 8192], P(('section', 'tp'), 'dp'), may hold values from -6 to 6
- weights: bfloat16 [4, 8192, 16384], P('section', 'dp', 'tp'), may hold values from -0.0625 to 0.0625
- readout: float32 [4, 16384], P('section', 'tp'), may hold values from -0.09375 to 0.09375
- lengths: int32 [16], replicated, may hold values from 1 to 256, 2048 in all
- groups: int32 [16], replicated, may hold values from 0 to 3
Outputs:
- weight_grad: bfloat16 [4, 2048, 16384], P('dp', 'section', 'tp')
- policy_loss: float32 [], replicated
Inputs may be any that keep to these rules, and one draw needn't show every extreme that they name: The lengths add up to 2048; the longest response has exactly 256 tokens.
All inputs are finite; a program needn't handle non-finite values.
Results may differ from a plain program's by a relative error of at most 0.005.
Values may be sent and summed in bfloat16 or wider, within the bound.
A program may use at most 64 MiB of HBM per device.

v0:
```python
import jax
import jax.numpy as jnp
from jax import lax
from jax.sharding import PartitionSpec as P

kl_weight = 0.2


def from_root(block, axis, source):
    block = jnp.where(lax.axis_index(axis) == source, block, jnp.zeros_like(block))
    return lax.psum(block, axis)


def advantages(rewards, groups):
    same_group = (groups[:, None] == groups[None, :]).astype(jnp.float32)
    members = jnp.sum(same_group, axis=1)
    group_mean = jnp.sum(same_group * rewards[None, :], axis=1) / members
    spread = jnp.sum(same_group * (rewards[None, :] - group_mean[:, None]) ** 2, axis=1) / members
    return (rewards - group_mean) / jnp.sqrt(spread + 1.0)


def contract_rows(left, right):
    return lax.dot_general(
        left, right, (((0,), (0,)), ((), ())), preferred_element_type=jnp.float32
    )


def local(responses, weights, readout, lengths, groups):
    gathered = lax.all_gather(responses, ("section", "tp"), axis=0, tiled=True)
    weight_block = weights[0]
    total_rows = gathered.shape[0]
    row_block = total_rows // lax.axis_size("dp")
    hidden = lax.psum_scatter(
        jnp.dot(gathered, weight_block, preferred_element_type=jnp.float32),
        "dp",
        scatter_dimension=0,
        tiled=True,
    )
    read_row = readout[0]
    partial_score = jnp.sum(jax.nn.silu(hidden) * read_row[None, :], axis=1)
    own_score = lax.psum(partial_score, "tp")
    joined = lax.all_gather(own_score[None, :], "section", axis=0, tiled=True)
    resp_count = lengths.shape[0]
    first_row = lax.axis_index("dp") * row_block
    position = first_row + jnp.arange(row_block, dtype=jnp.int32)
    starts = jnp.cumsum(lengths) - lengths
    finish = starts + lengths
    in_response = (
        (position[:, None] >= starts[None, :]) & (position[:, None] < finish[None, :])
    ).astype(jnp.float32)
    last_token = (position[:, None] == finish[None, :] - 1).astype(jnp.float32)
    token_len = jnp.sum(in_response * lengths.astype(jnp.float32)[None, :], axis=1)
    lp_old = jax.nn.log_sigmoid(joined[0])
    lp_ref = jax.nn.log_sigmoid(joined[1])
    lp_new = jax.nn.log_sigmoid(joined[3])
    prob_ratio = jnp.exp(lp_new - lp_old)
    log_gap = lp_ref - lp_new
    penalty = kl_weight * (jnp.exp(log_gap) - log_gap - 1.0)
    reward_part = jnp.sum(last_token * joined[2][:, None], axis=0)
    rewards = lax.psum(reward_part, "dp")
    advantage = advantages(rewards, groups)
    token_adv = jnp.sum(in_response * advantage[None, :], axis=1)
    token_loss = -prob_ratio * token_adv + penalty
    policy_loss = lax.psum(jnp.sum(token_loss / token_len), "dp") / resp_count
    coeff = (
        total_rows
        / (resp_count * token_len)
        * (-prob_ratio * token_adv + kl_weight * (1.0 - jnp.exp(log_gap)))
        * jax.nn.sigmoid(-joined[3])
    )
    sigmoid_z = jax.nn.sigmoid(hidden)
    silu_slope = sigmoid_z * (1.0 + hidden * (1.0 - sigmoid_z))
    hidden_grad = (coeff[:, None] * read_row[None, :] * silu_slope).astype(jnp.bfloat16)
    block_width = gathered.shape[1] // lax.axis_size("section")
    feature_block = lax.dynamic_slice_in_dim(
        gathered, lax.axis_index("section") * block_width, block_width, 1
    )
    learner_index = lax.axis_size("section") - 1
    all_grad = lax.all_gather(hidden_grad, "dp", axis=0, tiled=True)
    shared_grad = from_root(all_grad, "section", learner_index)
    weight_grad = contract_rows(feature_block, shared_grad)
    return (weight_grad.astype(jnp.bfloat16)[None], policy_loss)


def solution(mesh):
    return jax.shard_map(
        local,
        mesh=mesh,
        in_specs=(
            P(("section", "tp"), "dp"),
            P("section", "dp", "tp"),
            P("section", "tp"),
            P(),
            P(),
        ),
        out_specs=(P("dp", "section", "tp"), P()),
        check_vma=False,
    )
```

profile of v0, /device:TPU:1, one launch (start us, length us, event | category | flops | bytes accessed | tf_op | source)
XLA Modules:
  0.0 557.4 jit_solution(10904170529704305852)
XLA Ops:
  7.2 0.0 all-gather.4.cloned.1.call-start
  7.2 0.7 all-gather.4.cloned.1.call-update
  7.9 0.0 reduce-scatter.2.cloned.1.call-start
  7.9 120.6 %all-gather.4.cloned.1.call-done = bf16[2048,2048]{1,0:T(8,128)(2,1)} async-done(((bf16[32,2048]{1,0:T(8,128)(2,1)}), bf16[2048,2048]{1,0:T(8,128)(2,1)}) %all-gather.4.cloned.1.call-update) | async-done | bytes 8388624 | tf_op jit(solution)/shard_map/all_gather | solution.py:29
  128.5 14.4 %fusion = f32[2048,1024]{1,0:T(8,128)} fusion(bf16[2048,2048]{1,0:T(8,128)(2,1)} %all-gather.4.cloned.1.call-done, bf16[1,2048,1024]{2,1,0:T(8,128)(2,1)} %param.6), kind=kOutput, calls=%fused_computation | convolution fusion | flops 8589934592 | bytes 20971520 | tf_op jit(solution)/shard_map/dot_general | solution.py:34
  143.0 0.0 copy-start.3
  143.0 0.0 copy-start.1
  143.0 0.0 reduce-scatter.2.cloned.1.call-update
  143.0 0.0 copy-start.2
  143.0 0.0 all-gather.6.cloned.1.call-start
  143.1 0.6 copy-done.3
  143.6 0.1 copy.10
  143.7 0.1 reduce
  143.9 142.4 %reduce-scatter.2.cloned.1.call-done = f32[512,1024]{1,0:T(8,128)} async-done(((f32[2048,1024]{1,0:T(8,128)}), f32[512,1024]{1,0:T(8,128)}) %reduce-scatter.2.cloned.1.call-update) | async-done | bytes 2097168 | tf_op jit(solution)/shard_map/reduce_scatter | solution.py:33
  286.2 0.0 copy-start
  286.2 0.0 copy-done.1
  286.2 2.4 multiply_reduce_fusion
  288.6 43.0 %psum.28 = f32[1,512]{1,0:T(1,128)S(1)} all-reduce(f32[1,512]{1,0:T(1,128)S(1)} %bitcast.22), channel_id=1, replica_groups=mesh['section'=4,'tp'=16,'dp'=4] {'tp'}, use_global_device_ids=true, to_apply=%region_4.5 | all-reduce | flops 512 | bytes 4096 | tf_op jit(solution)/shard_map/psum | solution.py:41
  331.6 8.9 %all-gather = f32[4,1,512]{2,1,0:T(1,128)S(1)} all-gather(f32[1,1,512]{2,1,0:T(1,128)S(1)} %bitcast.25), channel_id=1, replica_groups=mesh['section'=4,'tp'=16,'dp'=4] {'section'}, dimensions={0}, use_global_device_ids=true | all-gather | bytes 10240 | tf_op jit(solution)/shard_map/all_gather | solution.py:42
  340.5 0.2 select_reduce_fusion.1
  340.7 9.4 %psum.29 = f32[16]{0:T(128)S(1)} all-reduce(f32[16]{0:T(128)S(1)} %select_reduce_fusion.1), channel_id=1, replica_groups=mesh['section'=4,'tp'=16,'dp'=4] {'dp'}, use_global_device_ids=true, to_apply=%region_6.7 | all-reduce | flops 16 | bytes 128 | tf_op jit(solution)/shard_map/psum | solution.py:60
  350.1 0.0 copy-done.2
  350.1 0.2 fusion.11
  350.3 0.2 fusion.12
  350.5 0.1 select_reduce_fusion.2
  350.6 0.6 fusion.28
  351.3 0.0 copy-done
  351.3 1.8 multiply_convert_fusion
  353.1 0.0 all-gather.6.cloned.1.call-update
  353.1 0.0 all-reduce.2.cloned.1.call-start
  353.1 88.0 %all-gather.6.cloned.1.call-done = bf16[2048,1024]{1,0:T(8,128)(2,1)} async-done(((bf16[512,1024]{1,0:T(8,128)(2,1)}), bf16[2048,1024]{1,0:T(8,128)(2,1)}) %all-gather.6.cloned.1.call-update) | async-done | bytes 4194320 | tf_op jit(solution)/shard_map/all_gather | solution.py:79
  441.2 2.2 broadcast_select_fusion
  443.4 0.0 all-reduce.2.cloned.1.call-update
  443.4 8.6 %psum.31 = f32[]{:T(128)} all-reduce(f32[]{:T(128)} %get-tuple-element.6), channel_id=1, replica_groups=mesh['section'=4,'tp'=16,'dp'=4] {'dp'}, use_global_device_ids=true, to_apply=%region_13.14 | all-reduce | flops 1 | bytes 8 | tf_op jit(solution)/shard_map/psum | solution.py:64
  452.7 90.9 %all-reduce.2.cloned.1.call-done = bf16[2048,1024]{1,0:T(8,128)(2,1)} async-done(((bf16[2048,1024]{1,0:T(8,128)(2,1)}), bf16[2048,1024]{1,0:T(8,128)(2,1)}) %all-reduce.2.cloned.1.call-update) | async-done | bytes 4194320 | tf_op jit(solution)/shard_map/psum | solution.py:11
  543.6 6.2 %fusion.7 = bf16[1,512,1024]{2,1,0:T(8,128)(2,1)} fusion(bf16[2048,1024]{1,0:T(8,128)(2,1)} %all-reduce.2.cloned.1.call-done, bf16[2048,2048]{1,0:T(8,128)(2,1)} %all-gather.4.cloned.1.call-done, s32[]{:T(128)S(6)} %select_n.34), kind=kOutput, calls=%fused_computation.9 | convolution fusion | flops 2148007936 | bytes 7340036 | tf_op jit(solution)/shard_map/dot_general | solution.py:23
  (7 shorter events, 0.1 us)
Async XLA Ops:
  7.2 121.4 %all-gather.4.cloned.1.call-start = ((), (), s32[]{:S(2)}) async-start(), calls=%async_computation.1 | async-start | bytes 8519680 | tf_op jit(solution)/shard_map/all_gather | solution.py:29
  7.9 278.3 %reduce-scatter.2.cloned.1.call-start = ((), (), s32[]{:S(2)}) async-start(), calls=%async_computation.2 | async-start | bytes 10485760 | tf_op jit(solution)/shard_map/reduce_scatter | solution.py:33
  143.0 0.7 copy-start.3
  143.0 143.3 %copy-start.1 = (f32[1,1024]{1,0:T(1,128)S(1)}, f32[1,1024]{1,0:T(1,128)}, u32[]{:S(2)}) copy-start(f32[1,1024]{1,0:T(1,128)} %param.7) | copy-start | bytes 12292
  143.0 207.1 %copy-start.2 = (s32[16]{0:T(128)S(1)}, s32[16]{0:T(128)}, u32[]{:S(2)}) copy-start(s32[16]{0:T(128)} %param.9) | copy-start | bytes 196
  143.0 298.2 %all-gather.6.cloned.1.call-start = ((), (), s32[]{:S(2)}) async-start(), calls=%async_computation.3 | async-start | bytes 5242880 | tf_op jit(solution)/shard_map/all_gather | solution.py:79
  286.2 65.0 %copy-start = (f32[512,1024]{1,0:T(8,128)S(1)}, f32[512,1024]{1,0:T(8,128)}, u32[]{:S(2)}) copy-start(f32[512,1024]{1,0:T(8,128)} %reduce-scatter.2.cloned.1.call-done) | copy-start | bytes 6291460
  353.1 190.5 %all-reduce.2.cloned.1.call-start = ((), (), s32[]{:S(2)}) async-start(), calls=%async_computation.4 | async-start | bytes 8388608 | tf_op jit(solution)/shard_map/psum | solution.py:11
Sparse Core Ops, SparseCore 0:
  11.5 117.0 all-gather.3
  143.1 143.0 reduce-scatter.1
  353.2 87.9 all-gather.5
  443.6 99.9 all-reduce.1
where the time goes:
time: 558 us; the launch traced here: 557 us
  waiting for transfers between devices  443 us (79%)
  blocking collectives  69.9 us (13%)
  matrix products  20.6 us (4%)
  between operations  15.6 us (3%)
  other arithmetic  7.89 us (1%)
    reduce_scatter x1, waiting for transfers between devices, local(): lax.psum_scatter(jnp.dot(gathered, weight_block, preferred_element_type=j...  142 us
    all_gather x1, waiting for transfers between devices, local(): gathered = lax.all_gather(responses, ('section', 'tp'), axis=0, tiled=True)  121 us
    psum x1, waiting for transfers between devices, from_root(): return lax.psum(block, axis)  90.9 us
    all_gather x1, waiting for transfers between devices, local(): all_grad = lax.all_gather(hidden_grad, 'dp', axis=0, tiled=True)  88 us
    psum x1, blocking collectives, local(): own_score = lax.psum(partial_score, 'tp')  43 us
    dot_general x1, matrix products, local(): jnp.dot(gathered, weight_block, preferred_element_type=jnp.float32)  14.4 us
  transfers between devices with their start and end apart: 4, of which 4 were waited for; matrix products, arithmetic and copies ran while one was open for 0% of the time, Pallas kernels for 0%

commit v1 on v0

--- a/solution.py
+++ b/solution.py
@@ -8,7 +8,7 @@
 
 def from_root(block, axis, source):
     block = jnp.where(lax.axis_index(axis) == source, block, jnp.zeros_like(block))
-    return lax.psum(block, axis)
+    return jnp.sum(lax.all_gather(block, axis), axis=0)
 
 
 def advantages(rewards, groups):

time: 558 us -> 629 us (1.13)
  waiting for transfers between devices: 443 us -> 501 us
  other arithmetic: 7.89 us -> 20 us
    all_gather x0 -> x1, waiting for transfers between devices: none -> 150 us  [from_root(): return jnp.sum(lax.all_gather(block, axis), axis=0)]
    psum x1 -> x0, waiting for transfers between devices: 90.9 us -> none  [from_root(): return lax.psum(block, axis)]
    reduce_sum x0 -> x1, other arithmetic: none -> 12.1 us  [from_root(): return jnp.sum(lax.all_gather(block, axis), axis=0)]
where the time goes in v1:
time: 629 us; the launch traced here: 628 us
  waiting for transfers between devices  501 us (80%)
  blocking collectives  69.8 us (11%)
  matrix products  20.6 us (3%)
  other arithmetic  20 us (3%)
  between operations  15.6 us (2%)
    all_gather x1, waiting for transfers between devices, from_root(): return jnp.sum(lax.all_gather(block, axis), axis=0)  150 us
    reduce_scatter x1, waiting for transfers between devices, local(): lax.psum_scatter(jnp.dot(gathered, weight_block, preferred_element_type=j...  142 us
    all_gather x1, waiting for transfers between devices, local(): gathered = lax.all_gather(responses, ('section', 'tp'), axis=0, tiled=True)  121 us
    all_gather x1, waiting for transfers between devices, local(): all_grad = lax.all_gather(hidden_grad, 'dp', axis=0, tiled=True)  88 us
    psum x1, blocking collectives, local(): own_score = lax.psum(partial_score, 'tp')  42.9 us
    dot_general x1, matrix products, local(): jnp.dot(gathered, weight_block, preferred_element_type=jnp.float32)  14.4 us
  transfers between devices with their start and end apart: 4, of which 4 were waited for; matrix products, arithmetic and copies ran while one was open for 0% of the time, Pallas kernels for 0%

profile of v1, /device:TPU:1, one launch (start us, length us, event | category | flops | bytes accessed | tf_op | source)
XLA Modules:
  0.0 628.3 jit_solution(10447645399820581998)
XLA Ops:
  7.2 0.0 all-gather.6.cloned.1.call-start
  7.2 0.7 all-gather.6.cloned.1.call-update
  7.9 0.0 reduce-scatter.2.cloned.1.call-start
  7.9 120.6 %all-gather.6.cloned.1.call-done = bf16[2048,2048]{1,0:T(8,128)(2,1)} async-done(((bf16[32,2048]{1,0:T(8,128)(2,1)}), bf16[2048,2048]{1,0:T(8,128)(2,1)}) %all-gather.6.cloned.1.call-update) | async-done | bytes 8388624 | tf_op jit(solution)/shard_map/all_gather | solution.py:29
  128.6 14.4 %fusion = f32[2048,1024]{1,0:T(8,128)} fusion(bf16[2048,2048]{1,0:T(8,128)(2,1)} %all-gather.6.cloned.1.call-done, bf16[1,2048,1024]{2,1,0:T(8,128)(2,1)} %param.6), kind=kOutput, calls=%fused_computation | convolution fusion | flops 8589934592 | bytes 20971520 | tf_op jit(solution)/shard_map/dot_general | solution.py:34
  143.0 0.0 copy-start.3
  143.0 0.0 copy-start.1
  143.0 0.0 reduce-scatter.2.cloned.1.call-update
  143.0 0.0 copy-start.2
  143.0 0.0 all-gather.8.cloned.1.call-start
  143.1 0.6 copy-done.3
  143.7 0.1 copy.10
  143.8 0.1 reduce.1
  143.9 142.4 %reduce-scatter.2.cloned.1.call-done = f32[512,1024]{1,0:T(8,128)} async-done(((f32[2048,1024]{1,0:T(8,128)}), f32[512,1024]{1,0:T(8,128)}) %reduce-scatter.2.cloned.1.call-update) | async-done | bytes 2097168 | tf_op jit(solution)/shard_map/reduce_scatter | solution.py:33
  286.3 0.0 copy-start
  286.3 0.0 copy-done.1
  286.3 2.4 multiply_reduce_fusion
  288.7 42.9 %psum.21 = f32[1,512]{1,0:T(1,128)S(1)} all-reduce(f32[1,512]{1,0:T(1,128)S(1)} %bitcast.24), channel_id=1, replica_groups=mesh['section'=4,'tp'=16,'dp'=4] {'tp'}, use_global_device_ids=true, to_apply=%region_4.5 | all-reduce | flops 512 | bytes 4096 | tf_op jit(solution)/shard_map/psum | solution.py:41
  331.6 8.9 %all-gather.1 = f32[4,1,512]{2,1,0:T(1,128)S(1)} all-gather(f32[1,1,512]{2,1,0:T(1,128)S(1)} %bitcast.27), channel_id=1, replica_groups=mesh['section'=4,'tp'=16,'dp'=4] {'section'}, dimensions={0}, use_global_device_ids=true | all-gather | bytes 10240 | tf_op jit(solution)/shard_map/all_gather | solution.py:42
  340.5 0.2 select_reduce_fusion.1
  340.7 9.4 %psum.22 = f32[16]{0:T(128)S(1)} all-reduce(f32[16]{0:T(128)S(1)} %select_reduce_fusion.1), channel_id=1, replica_groups=mesh['section'=4,'tp'=16,'dp'=4] {'dp'}, use_global_device_ids=true, to_apply=%region_6.7 | all-reduce | flops 16 | bytes 128 | tf_op jit(solution)/shard_map/psum | solution.py:60
  350.2 0.0 copy-done.2
  350.2 0.2 fusion.11
  350.4 0.2 fusion.12
  350.6 0.1 select_reduce_fusion.2
  350.7 0.6 fusion.28
  351.3 0.0 copy-done
  351.3 1.8 multiply_convert_fusion
  353.1 0.0 all-gather.8.cloned.1.call-update
  353.1 0.0 all-gather.10.cloned.1.call-start
  353.2 88.0 %all-gather.8.cloned.1.call-done = bf16[2048,1024]{1,0:T(8,128)(2,1)} async-done(((bf16[512,1024]{1,0:T(8,128)(2,1)}), bf16[2048,1024]{1,0:T(8,128)(2,1)}) %all-gather.8.cloned.1.call-update) | async-done | bytes 4194320 | tf_op jit(solution)/shard_map/all_gather | solution.py:79
  441.2 2.3 broadcast_select_fusion
  443.5 0.0 all-gather.10.cloned.1.call-update
  443.5 8.6 %psum.23 = f32[]{:T(128)} all-reduce(f32[]{:T(128)} %get-tuple-element.6), channel_id=1, replica_groups=mesh['section'=4,'tp'=16,'dp'=4] {'dp'}, use_global_device_ids=true, to_apply=%region_13.14 | all-reduce | flops 1 | bytes 8 | tf_op jit(solution)/shard_map/psum | solution.py:64
  452.7 149.7 %all-gather.10.cloned.1.call-done = bf16[8192,1024]{1,0:T(8,128)(2,1)} async-done(((bf16[2048,1024]{1,0:T(8,128)(2,1)}), bf16[8192,1024]{1,0:T(8,128)(2,1)}) %all-gather.10.cloned.1.call-update) | async-done | bytes 16777232 | tf_op jit(solution)/shard_map/all_gather | solution.py:11
  602.4 12.1 %reduce_sum.91 = bf16[2048,1024]{1,0:T(8,128)(2,1)} reduce(bf16[4,2048,1024]{2,1,0:T(8,128)(2,1)} %bitcast.17, bf16[]{:T(256)} %constant.51.clone.1), dimensions={0}, to_apply=%region_11.12 | reduce | flops 6291456 | bytes 20971522 | tf_op jit(solution)/shard_map/reduce_sum | solution.py:11
  614.5 6.2 fusion.7
  (7 shorter events, 0.1 us)
Async XLA Ops:
  7.2 121.4 %all-gather.6.cloned.1.call-start = ((), (), s32[]{:S(2)}) async-start(), calls=%async_computation.1 | async-start | bytes 8519680 | tf_op jit(solution)/shard_map/all_gather | solution.py:29
  7.9 278.4 %reduce-scatter.2.cloned.1.call-start = ((), (), s32[]{:S(2)}) async-start(), calls=%async_computation.2 | async-start | bytes 10485760 | tf_op jit(solution)/shard_map/reduce_scatter | solution.py:33
  143.0 0.7 copy-start.3
  143.0 143.3 %copy-start.1 = (f32[1,1024]{1,0:T(1,128)S(1)}, f32[1,1024]{1,0:T(1,128)}, u32[]{:S(2)}) copy-start(f32[1,1024]{1,0:T(1,128)} %param.7) | copy-start | bytes 12292
  143.0 207.1 %copy-start.2 = (s32[16]{0:T(128)S(1)}, s32[16]{0:T(128)}, u32[]{:S(2)}) copy-start(s32[16]{0:T(128)} %param.9) | copy-start | bytes 196
  143.0 298.2 %all-gather.8.cloned.1.call-start = ((), (), s32[]{:S(2)}) async-start(), calls=%async_computation.3 | async-start | bytes 5242880 | tf_op jit(solution)/shard_map/all_gather | solution.py:79
  286.3 65.0 %copy-start = (f32[512,1024]{1,0:T(8,128)S(1)}, f32[512,1024]{1,0:T(8,128)}, u32[]{:S(2)}) copy-start(f32[512,1024]{1,0:T(8,128)} %reduce-scatter.2.cloned.1.call-done) | copy-start | bytes 6291460
  353.1 249.3 %all-gather.10.cloned.1.call-start = ((), (), s32[]{:S(2)}) async-start(), calls=%async_computation.4 | async-start | bytes 20971520 | tf_op jit(solution)/shard_map/all_gather | solution.py:11
Sparse Core Ops, SparseCore 0:
  11.5 117.0 all-gather.5
  143.1 143.1 reduce-scatter.1
  353.2 87.9 all-gather.7
  443.6 158.7 all-gather.9
